TPU v7x, 32 devices: a whole 2x2x4 slice. The times are simulated.
32 devices in a mesh: row: 8 (over z, x), col: 4 (over y, core).
Axes of the slice: x: 2, y: 2, z: 4, core: 2. Of those that a mesh axis runs over, the one named last changes fastest.
Arguments:
- momentum: bfloat16 [16384, 16384], P('row', 'col'), may hold values from -16 to 16
- gradient: bfloat16 [16384, 16384], P('row', 'col'), may hold values from -6 to 6
- right_basis: bfloat16 [1024, 16384], P('row', 'col'), may hold values from -1 to 1
Outputs:
- momentum_next: bfloat16 [16384, 16384], P('row', 'col')
- basis_next: float32 [1024, 16384], P('row', 'col')
- update: bfloat16 [16384, 16384], P('row', 'col')
All inputs are finite; a program needn't handle non-finite values.
Results may differ from a plain program's by a relative error of at most 0.02.
Values may be sent and summed in bfloat16 or wider, within the bound.
A program may use at most 128 MiB of HBM per device.

v0:
```python
import math
import jax
import jax.numpy as jnp
from jax import lax
from jax.sharding import PartitionSpec as P

D = 16384
RANK = 1024
momentum_decay = 0.95
epsilon = 1e-06


def orthonormalize(projected, gram_matrix):
    lower_factor = jnp.linalg.cholesky(gram_matrix)
    solved = jax.scipy.linalg.solve_triangular(lower_factor, projected.T, lower=True)
    return solved.T.astype(jnp.bfloat16)


def self_gram(projected):
    return lax.dot_general(
        projected, projected, (((0,), (0,)), ((), ())), precision=lax.Precision.HIGHEST
    )


def body(momentum, gradient, right_basis):
    buffer = (momentum.astype(jnp.float32) + gradient.astype(jnp.float32)).astype(jnp.bfloat16)
    rank_rows = right_basis.shape[0]
    partial_value = lax.dot_general(
        buffer,
        lax.all_gather(right_basis, "row", axis=0, tiled=True),
        (((1,), (1,)), ((), ())),
        preferred_element_type=jnp.float32,
    )
    row_share = lax.psum_scatter(
        partial_value.astype(jnp.bfloat16), "col", scatter_dimension=0, tiled=True
    ).astype(jnp.float32)
    gram_matrix = lax.psum(self_gram(row_share), ("row", "col"))
    ortho_share = orthonormalize(row_share, gram_matrix)
    orthonormal = lax.all_gather(ortho_share, "col", axis=0, tiled=True)
    right_share = lax.psum_scatter(
        lax.dot_general(
            orthonormal, buffer, (((0,), (0,)), ((), ())), preferred_element_type=jnp.float32
        ).astype(jnp.bfloat16),
        "row",
        scatter_dimension=0,
        tiled=True,
    )
    right_wide = right_share.astype(jnp.float32)
    gathered = lax.all_gather(right_share, "row", axis=0, tiled=True)
    gathered_wide = gathered.astype(jnp.float32)
    sums_total = lax.psum(jnp.sum(gathered_wide * gathered_wide, axis=1), "col")
    inverse_norm = lax.rsqrt(sums_total + epsilon)[:, None]
    scaled = (gathered_wide * inverse_norm).astype(jnp.bfloat16)
    feedback = jnp.dot(orthonormal, gathered, preferred_element_type=jnp.float32)
    direction = jnp.dot(orthonormal, scaled, preferred_element_type=jnp.float32)
    offset = lax.axis_index("row") * rank_rows
    basis_next = right_wide * lax.dynamic_slice_in_dim(inverse_norm, offset, rank_rows, 0)
    momentum_next = (buffer.astype(jnp.float32) - (1.0 - momentum_decay) * feedback).astype(
        jnp.bfloat16
    )
    update_scale = D / math.sqrt(RANK)
    update = (update_scale * direction).astype(jnp.bfloat16)
    return (momentum_next, basis_next, update)


def solution(mesh):
    return jax.shard_map(
        body,
        mesh=mesh,
        in_specs=(P("row", "col"), P("row", "col"), P("row", "col")),
        out_specs=(P("row", "col"), P("row", "col"), P("row", "col")),
        check_vma=False,
    )
```

profile of v0, /device:TPU:0, one launch (start us, length us, event | category | flops | bytes accessed | tf_op | source)
XLA Modules:
  0.0 1132.3 jit_solution(6209591932826324028)
XLA Ops:
  7.9 129.4 %all-gather.4.cloned.1.call-done = bf16[1024,4096]{1,0:T(8,128)(2,1)} async-done(((bf16[128,4096]{1,0:T(8,128)(2,1)}), bf16[1024,4096]{1,0:T(8,128)(2,1)}) %all-gather.4.cloned.1.call-update) | async-done | bytes 8388624 | tf_op jit(solution)/shard_map/all_gather | solution.py:30
  137.3 25.8 %convolution_convert_fusion.1 = bf16[2048,1024]{1,0:T(8,128)(2,1)} fusion(bf16[1024,4096]{1,0:T(8,128)(2,1)} %all-gather.4.cloned.1.call-done, bf16[2048,4096]{1,0:T(8,128)(2,1)} %param.4, bf16[2048,4096]{1,0:T(8,128)(2,1)} %param.3), kind=kOutput, calls=%fused_computation.15 | convolution fusion | flops 17215520768 | bytes 46137344 | tf_op jit(solution)/shard_map/dot_general | solution.py:28
  163.2 42.9 %reduce-scatter.3.cloned.1.call-done = bf16[512,1024]{1,0:T(8,128)(2,1)} async-done(((bf16[2048,1024]{1,0:T(8,128)(2,1)}), bf16[512,1024]{1,0:T(8,128)(2,1)}) %reduce-scatter.3.cloned.1.call-update) | async-done | bytes 1048592 | tf_op jit(solution)/shard_map/reduce_scatter | solution.py:34
  206.1 4.9 fusion.67
  211.3 143.2 %all-reduce.3.cloned.1.call-done = f32[1024,1024]{0,1:T(8,128)} async-done(((f32[1024,1024]{0,1:T(8,128)}), f32[1024,1024]{0,1:T(8,128)}) %all-reduce.3.cloned.1.call-update) | async-done | bytes 4194320 | tf_op jit(solution)/shard_map/psum | solution.py:37
  354.5 5.5 copy.7
  360.0 4.4 fusion.4
  366.5 11.7 %cholesky.223 = f32[128,128]{1,0:T(8,128)S(1)} custom-call(f32[128,128]{1,0:T(8,128)S(1)} %cholesky.580), custom_call_target="Cholesky" | custom-call | tf_op jit(solution)/shard_map/jit(cholesky)/cholesky | solution.py:14
  378.2 9.8 custom-call.63
  388.1 2.5 cholesky.255
  395.2 12.1 %cholesky.244 = f32[128,128]{1,0:T(8,128)S(1)} custom-call(f32[128,128]{1,0:T(8,128)S(1)} %cholesky.584), custom_call_target="Cholesky" | custom-call | tf_op jit(solution)/shard_map/jit(cholesky)/cholesky | solution.py:14
  408.0 9.8 custom-call.64
  422.7 13.2 %cholesky.468 = f32[128,128]{1,0:T(8,128)} custom-call(f32[128,128]{1,0:T(8,128)} %cholesky.589), custom_call_target="Cholesky" | custom-call | tf_op jit(solution)/shard_map/jit(cholesky)/cholesky | solution.py:14
  438.0 11.3 custom-call.65
  451.2 2.3 convolution_subtract_fusion.2
  453.6 12.5 %cholesky.487 = f32[128,128]{1,0:T(8,128)} custom-call(f32[128,128]{1,0:T(8,128)S(1)} %cholesky.594), custom_call_target="Cholesky" | custom-call | tf_op jit(solution)/shard_map/jit(cholesky)/cholesky | solution.py:14
  468.2 10.4 custom-call.66
  482.9 11.7 %cholesky.506 = f32[128,128]{1,0:T(8,128)S(1)} custom-call(f32[128,128]{1,0:T(8,128)S(1)} %cholesky.599), custom_call_target="Cholesky" | custom-call | tf_op jit(solution)/shard_map/jit(cholesky)/cholesky | solution.py:14
  495.9 10.0 custom-call.67
  509.2 11.7 %cholesky.526 = f32[128,128]{1,0:T(8,128)S(1)} custom-call(f32[128,128]{1,0:T(8,128)S(1)} %cholesky.604), custom_call_target="Cholesky" | custom-call | tf_op jit(solution)/shard_map/jit(cholesky)/cholesky | solution.py:14
  522.2 9.8 custom-call.68
  535.0 12.0 %cholesky.546 = f32[128,128]{1,0:T(8,128)S(1)} custom-call(f32[128,128]{1,0:T(8,128)S(1)} %cholesky.609), custom_call_target="Cholesky" | custom-call | tf_op jit(solution)/shard_map/jit(cholesky)/cholesky | solution.py:14
  548.4 9.8 custom-call.69
  560.9 11.7 %cholesky.564 = f32[128,128]{1,0:T(8,128)S(1)} custom-call(f32[128,128]{1,0:T(8,128)S(1)} %convolution_subtract_fusion.13), custom_call_target="Cholesky" | custom-call | tf_op jit(solution)/shard_map/jit(cholesky)/cholesky | solution.py:14
  579.5 4.9 select_select_fusion
  584.4 29.0 %while.1 = (s32[]{:T(128)}, f32[1024,1024]{1,0:T(8,128)}, s32[8,2]{0,1:T(2,128)S(1)}, f32[8,128,128]{2,1,0:T(8,128)}, s32[]{:T(128)}) while((s32[]{:T(128)}, f32[1024,1024]{1,0:T(8,128)}, s32[8,2]{0,1:T(2,128)S(1)}, f32[8,128,128]{2,1,0:T(8,128)}, s32[]{:T(128)}) %tuple.57), condition=%wide.while_cond, body=%wide.while_body.sunk | while | flops 2 | bytes 132205 | solution.py:15
  585.1 3.0 bitcast_dynamic-update-slice_fusion.2
  588.7 3.0 bitcast_dynamic-update-slice_fusion.2
  592.3 3.0 bitcast_dynamic-update-slice_fusion.2
  596.0 3.0 bitcast_dynamic-update-slice_fusion.2
  599.6 3.0 bitcast_dynamic-update-slice_fusion.2
  603.2 3.0 bitcast_dynamic-update-slice_fusion.2
  606.9 3.0 bitcast_dynamic-update-slice_fusion.2
  610.5 2.9 bitcast_dynamic-update-slice_fusion.2
  613.4 80.2 %custom-call.70 = f32[8,128,128]{1,2,0:T(8,128)} custom-call(f32[8,128,128]{2,1,0:T(8,128)} %get-tuple-element.10), custom_call_target="InvertDiagBlocksLowerTriangular" | custom-call | tf_op jit(solution)/shard_map/jit(_solve_triangular)/triangular_solve | solution.py:15
  702.0 2.4 convolution_subtract_fusion.8
  705.4 2.8 convolution_subtract_fusion.9
  709.7 3.2 convolution_subtract_fusion.4
  714.0 3.6 convolution_subtract_fusion.7
  718.8 4.3 convolution_subtract_fusion.3
  724.2 33.9 %all-gather.6.cloned.1.call-done = bf16[2048,1024]{0,1:T(8,128)(2,1)} async-done(((bf16[512,1024]{0,1:T(8,128)(2,1)}), bf16[2048,1024]{0,1:T(8,128)(2,1)}) %all-gather.6.cloned.1.call-update) | async-done | bytes 4194320 | tf_op jit(solution)/shard_map/all_gather | solution.py:39
  758.1 24.2 %convolution_convert_fusion = bf16[1024,4096]{1,0:T(8,128)(2,1)} fusion(bf16[2048,1024]{0,1:T(8,128)(2,1)} %all-gather.6.cloned.1.call-done, bf16[2048,4096]{1,0:T(8,128)(2,1)} %param.4, bf16[2048,4096]{1,0:T(8,128)(2,1)} %param.3), kind=kOutput, calls=%fused_computation.10 | convolution fusion | flops 17217617920 | bytes 46137344 | tf_op jit(solution)/shard_map/dot_general | solution.py:41
  782.3 147.5 %reduce-scatter.5.cloned.1.call-done = bf16[128,4096]{1,0:T(8,128)(2,1)} async-done(((bf16[1024,4096]{1,0:T(8,128)(2,1)}), bf16[128,4096]{1,0:T(8,128)(2,1)}) %reduce-scatter.5.cloned.1.call-update) | async-done | bytes 1048592 | tf_op jit(solution)/shard_map/reduce_scatter | solution.py:40
  929.9 125.6 %all-gather.8.cloned.1.call-done = bf16[1024,4096]{1,0:T(8,128)(2,1)} async-done(((bf16[128,4096]{1,0:T(8,128)(2,1)}), bf16[1024,4096]{1,0:T(8,128)(2,1)}) %all-gather.8.cloned.1.call-update) | async-done | bytes 8388624 | tf_op jit(solution)/shard_map/all_gather | solution.py:49
  1055.5 5.1 fusion
  1060.5 5.9 psum.15
  1066.5 26.4 %multiply_convert_fusion = bf16[2048,4096]{1,0:T(8,128)(2,1)} fusion(bf16[2048,1024]{0,1:T(8,128)(2,1)} %all-gather.6.cloned.1.call-done, bf16[1024,4096]{1,0:T(8,128)(2,1)} %all-gather.8.cloned.1.call-done, f32[1024]{0:T(1024)S(1)} %add_rsqrt_fusion), kind=kOutput, calls=%fused_computation.2 | convolution fusion | flops 17209229312 | bytes 29364224 | tf_op jit(solution)/shard_map/dot_general | solution.py:55
  1092.9 30.5 %subtract_convert_fusion = bf16[2048,4096]{1,0:T(8,128)(2,1)} fusion(bf16[2048,1024]{0,1:T(8,128)(2,1)S(1)} %copy-done.5, bf16[1024,4096]{1,0:T(8,128)(2,1)} %all-gather.8.cloned.1.call-done, bf16[2048,4096]{1,0:T(8,128)(2,1)} %param.4, bf16[2048,4096]{1,0:T(8,128)(2,1)} %param.3), kind=kOutput, calls=%fused_computation.3 | convolution fusion | flops 17246978048 | bytes 62914560 | tf_op jit(solution)/shard_map/dot_general | solution.py:54
  (99 shorter events, 59.9 us)
Async XLA Ops:
  7.2 130.2 %all-gather.4.cloned.1.call-start = ((), (), s32[]{:S(2)}) async-start(), calls=%async_computation.2 | async-start | bytes 9437184 | tf_op jit(solution)/shard_map/all_gather | solution.py:30
  7.9 198.2 %reduce-scatter.3.cloned.1.call-start = ((), (), s32[]{:S(2)}) async-start(), calls=%async_computation.3 | async-start | bytes 5242880 | tf_op jit(solution)/shard_map/reduce_scatter | solution.py:34
  163.1 191.4 %all-reduce.3.cloned.1.call-start = ((), (), s32[]{:S(2)}) async-start(), calls=%async_computation.4 | async-start | bytes 8388608 | tf_op jit(solution)/shard_map/psum | solution.py:37
  206.1 5.0 copy-start
  211.0 547.1 %all-gather.6.cloned.1.call-start = ((), (), s32[]{:S(2)}) async-start(), calls=%async_computation.5 | async-start | bytes 5242880 | tf_op jit(solution)/shard_map/all_gather | solution.py:39
  364.5 2.0 copy-start.1
  394.5 0.8 copy-start.3
  693.6 7.2 copy-start.4
  724.2 205.7 %reduce-scatter.5.cloned.1.call-start = ((), (), s32[]{:S(2)}) async-start(), calls=%async_computation.6 | async-start | bytes 9437184 | tf_op jit(solution)/shard_map/reduce_scatter | solution.py:40
  782.3 273.2 %all-gather.8.cloned.1.call-start = ((), (), s32[]{:S(2)}) async-start(), calls=%async_computation.7 | async-start | bytes 9437184 | tf_op jit(solution)/shard_map/all_gather | solution.py:49
  1066.5 26.4 %copy-start.5 = (bf16[2048,1024]{0,1:T(8,128)(2,1)S(1)}, bf16[2048,1024]{0,1:T(8,128)(2,1)}, u32[]{:S(2)}) copy-start(bf16[2048,1024]{0,1:T(8,128)(2,1)} %all-gather.6.cloned.1.call-done) | copy-start | bytes 12582916
  1092.9 30.5 %copy-start.2 = (bf16[128,4096]{1,0:T(8,128)(2,1)S(1)}, bf16[128,4096]{1,0:T(8,128)(2,1)}, u32[]{:S(2)}) copy-start(bf16[128,4096]{1,0:T(8,128)(2,1)} %reduce-scatter.5.cloned.1.call-done) | copy-start | bytes 3145732
Sparse Core Ops, SparseCore 0:
  10.1 127.1 all-gather.3
  163.3 42.7 reduce-scatter.2
  212.2 142.2 all-reduce.2
  724.3 33.7 all-gather.5
  782.4 147.4 reduce-scatter.4
  931.9 123.5 all-gather.7
where the time goes:
time: 1140 us; the launch traced here: 1130 us
  waiting for transfers between devices  623 us (55%)
  other arithmetic  275 us (24%)
  matrix products  167 us (15%)
  local copies, waits for them, and re-layouts  41.1 us (4%)
  between operations  19.9 us (2%)
    another operation x30, other arithmetic, orthonormalize(): lower_factor = jnp.linalg.cholesky(gram_matrix)  178 us
    reduce_scatter x1, waiting for transfers between devices, body(): lax.psum_scatter(lax.dot_general(orthonormal, buffer, (((0,), (0,)), ((),...  148 us
    psum x1, waiting for transfers between devices, body(): gram_matrix = lax.psum(self_gram(row_share), ('row', 'col'))  143 us
    all_gather x1, waiting for transfers between devices, body(): lax.all_gather(right_basis, 'row', axis=0, tiled=True)  129 us
    all_gather x1, waiting for transfers between devices, body(): gathered = lax.all_gather(right_share, 'row', axis=0, tiled=True)  126 us
    another operation x3, other arithmetic, orthonormalize(): jax.scipy.linalg.solve_triangular(lower_factor, projected.T, lower=True)  85.1 us
    reduce_scatter x1, waiting for transfers between devices, body(): lax.psum_scatter(partial_value.astype(jnp.bfloat16), 'col', scatter_dimen...  42.9 us
    all_gather x1, waiting for transfers between devices, body(): orthonormal = lax.all_gather(ortho_share, 'col', axis=0, tiled=True)  33.9 us
  transfers between devices with their start and end apart: 6, of which 6 were waited for; matrix products, arithmetic and copies ran while one was open for 0% of the time, Pallas kernels for 0%

commit v1 on v0

--- a/solution.py
+++ b/solution.py
@@ -46,7 +46,26 @@
         tiled=True,
     )
     right_wide = right_share.astype(jnp.float32)
-    gathered = lax.all_gather(right_share, "row", axis=0, tiled=True)
+    size, position, span = (lax.axis_size("row"), lax.axis_index("row"), right_share.shape[0])
+    ahead = [(i, (i + 1) % size) for i in range(size)]
+    downward = [(i, (i - 1) % size) for i in range(size)]
+    out = jnp.zeros(
+        (*right_share.shape[:0], size * span, *right_share.shape[0 + 1 :]), right_share.dtype
+    )
+    out = lax.dynamic_update_slice_in_dim(out, right_share, position * span, axis=0)
+    from_left = from_right = right_share
+    half = size // 2
+    for step in range(1, half + 1):
+        from_left = lax.ppermute(from_left, "row", ahead)
+        out = lax.dynamic_update_slice_in_dim(
+            out, from_left, (position - step) % size * span, axis=0
+        )
+        if step < size - half:
+            from_right = lax.ppermute(from_right, "row", downward)
+            out = lax.dynamic_update_slice_in_dim(
+                out, from_right, (position + step) % size * span, axis=0
+            )
+    gathered = out
     gathered_wide = gathered.astype(jnp.float32)
     sums_total = lax.psum(jnp.sum(gathered_wide * gathered_wide, axis=1), "col")
     inverse_norm = lax.rsqrt(sums_total + epsilon)[:, None]

time: 1140 us -> 1180 us (1.035)
  waiting for transfers between devices: 623 us -> 645 us
  starting transfers between devices: 0.24 us -> 16.9 us
    ppermute x0 -> x7, waiting for transfers between devices: none -> 146 us  [the longest x4 146 us: body(): from_left = lax.ppermute(from_left, 'row', ahead)]
    all_gather x1 -> x0, waiting for transfers between devices: 126 us -> none  [body(): gathered = lax.all_gather(right_share, 'row', axis=0, tiled=True)]
    ppermute x0 -> x7, starting transfers between devices: none -> 16.7 us  [the longest x4 8.83 us: body(): from_left = lax.ppermute(from_left, 'row', ahead)]
  transfers between devices with their start and end apart: 6 -> 12, of which waited for: 6 -> 10; matrix products, arithmetic and copies ran while one was open for 0% -> 0% of each run, Pallas kernels for 0% -> 0%
where the time goes in v1:
time: 1180 us; the launch traced here: 1170 us
  waiting for transfers between devices  645 us (55%)
  other arithmetic  271 us (23%)
  matrix products  168 us (14%)
  local copies, waits for them, and re-layouts  47.7 us (4%)
  between operations  19.4 us (2%)
  starting transfers between devices  16.9 us (1%)
    another operation x30, other arithmetic, orthonormalize(): lower_factor = jnp.linalg.cholesky(gram_matrix)  178 us
    reduce_scatter x1, waiting for transfers between devices, body(): lax.psum_scatter(lax.dot_general(orthonormal, buffer, (((0,), (0,)), ((),...  148 us
    ppermute x4, waiting for transfers between devices, body(): from_left = lax.ppermute(from_left, 'row', ahead)  146 us
    psum x1, waiting for transfers between devices, body(): gram_matrix = lax.psum(self_gram(row_share), ('row', 'col'))  143 us
    all_gather x1, waiting for transfers between devices, body(): lax.all_gather(right_basis, 'row', axis=0, tiled=True)  129 us
    another operation x3, other arithmetic, orthonormalize(): jax.scipy.linalg.solve_triangular(lower_factor, projected.T, lower=True)  85.1 us
    reduce_scatter x1, waiting for transfers between devices, body(): lax.psum_scatter(partial_value.astype(jnp.bfloat16), 'col', scatter_dimen...  42.9 us
    all_gather x1, waiting for transfers between devices, body(): orthonormal = lax.all_gather(ortho_share, 'col', axis=0, tiled=True)  33.9 us
  transfers between devices with their start and end apart: 12, of which 10 were waited for; matrix products, arithmetic and copies ran while one was open for 0% of the time, Pallas kernels for 0%

profile of v1, /device:TPU:0, one launch (start us, length us, event | category | flops | bytes accessed | tf_op | source)
XLA Modules:
  0.0 1173.1 jit_solution(13412257922681826083)
XLA Ops:
  7.9 129.4 %all-gather.3.cloned.1.call-done = bf16[1024,4096]{1,0:T(8,128)(2,1)} async-done(((bf16[128,4096]{1,0:T(8,128)(2,1)}), bf16[1024,4096]{1,0:T(8,128)(2,1)}) %all-gather.3.cloned.1.call-update) | async-done | bytes 8388624 | tf_op jit(solution)/shard_map/all_gather | solution.py:30
  137.3 25.8 %convolution_convert_fusion.1 = bf16[2048,1024]{1,0:T(8,128)(2,1)} fusion(bf16[1024,4096]{1,0:T(8,128)(2,1)} %all-gather.3.cloned.1.call-done, bf16[2048,4096]{1,0:T(8,128)(2,1)} %param.4, bf16[2048,4096]{1,0:T(8,128)(2,1)} %param.3), kind=kOutput, calls=%fused_computation.15 | convolution fusion | flops 17215520768 | bytes 46137344 | tf_op jit(solution)/shard_map/dot_general | solution.py:28
  163.2 42.9 %reduce-scatter.3.cloned.1.call-done = bf16[512,1024]{1,0:T(8,128)(2,1)} async-done(((bf16[2048,1024]{1,0:T(8,128)(2,1)}), bf16[512,1024]{1,0:T(8,128)(2,1)}) %reduce-scatter.3.cloned.1.call-update) | async-done | bytes 1048592 | tf_op jit(solution)/shard_map/reduce_scatter | solution.py:34
  206.1 4.9 fusion.67
  211.3 143.3 %all-reduce.3.cloned.1.call-done = f32[1024,1024]{0,1:T(8,128)} async-done(((f32[1024,1024]{0,1:T(8,128)}), f32[1024,1024]{0,1:T(8,128)}) %all-reduce.3.cloned.1.call-update) | async-done | bytes 4194320 | tf_op jit(solution)/shard_map/psum | solution.py:37
  354.7 5.8 copy.7
  360.5 4.4 fusion.4
  366.9 11.7 cholesky.223
  378.7 9.8 custom-call.63
  395.7 11.9 %cholesky.244 = f32[128,128]{1,0:T(8,128)S(1)} custom-call(f32[128,128]{1,0:T(8,128)S(1)} %cholesky.584), custom_call_target="Cholesky" | custom-call | tf_op jit(solution)/shard_map/jit(cholesky)/cholesky | solution.py:14
  408.2 9.8 custom-call.64
  422.9 13.2 %cholesky.468 = f32[128,128]{1,0:T(8,128)} custom-call(f32[128,128]{1,0:T(8,128)} %cholesky.589), custom_call_target="Cholesky" | custom-call | tf_op jit(solution)/shard_map/jit(cholesky)/cholesky | solution.py:14
  438.2 11.3 custom-call.65
  453.8 12.5 %cholesky.487 = f32[128,128]{1,0:T(8,128)} custom-call(f32[128,128]{1,0:T(8,128)S(1)} %cholesky.594), custom_call_target="Cholesky" | custom-call | tf_op jit(solution)/shard_map/jit(cholesky)/cholesky | solution.py:14
  468.5 10.4 custom-call.66
  483.2 11.7 cholesky.506
  496.2 10.2 custom-call.67
  509.6 11.7 cholesky.526
  522.6 9.8 custom-call.68
  535.5 11.8 %cholesky.546 = f32[128,128]{1,0:T(8,128)S(1)} custom-call(f32[128,128]{1,0:T(8,128)S(1)} %cholesky.609), custom_call_target="Cholesky" | custom-call | tf_op jit(solution)/shard_map/jit(cholesky)/cholesky | solution.py:14
  548.6 9.8 custom-call.69
  561.1 11.7 cholesky.564
  579.7 4.9 select_select_fusion
  584.6 29.0 %while.1 = (s32[]{:T(128)}, f32[1024,1024]{1,0:T(8,128)}, s32[8,2]{0,1:T(2,128)S(1)}, f32[8,128,128]{2,1,0:T(8,128)}, s32[]{:T(128)}) while((s32[]{:T(128)}, f32[1024,1024]{1,0:T(8,128)}, s32[8,2]{0,1:T(2,128)S(1)}, f32[8,128,128]{2,1,0:T(8,128)}, s32[]{:T(128)}) %tuple.57), condition=%wide.while_cond, body=%wide.while_body.sunk | while | flops 2 | bytes 132205 | solution.py:15
  585.3 3.0 bitcast_dynamic-update-slice_fusion.2
  588.9 3.0 bitcast_dynamic-update-slice_fusion.2
  592.5 3.0 bitcast_dynamic-update-slice_fusion.2
  596.2 3.0 bitcast_dynamic-update-slice_fusion.2
  599.8 3.0 bitcast_dynamic-update-slice_fusion.2
  603.4 3.0 bitcast_dynamic-update-slice_fusion.2
  607.1 3.0 bitcast_dynamic-update-slice_fusion.2
  610.7 2.9 bitcast_dynamic-update-slice_fusion.2
  613.6 80.2 %custom-call.70 = f32[8,128,128]{1,2,0:T(8,128)} custom-call(f32[8,128,128]{2,1,0:T(8,128)} %get-tuple-element.10), custom_call_target="InvertDiagBlocksLowerTriangular" | custom-call | tf_op jit(solution)/shard_map/jit(_solve_triangular)/triangular_solve | solution.py:15
  709.9 3.2 convolution_subtract_fusion.4
  714.3 3.6 convolution_subtract_fusion.7
  719.0 4.5 convolution_subtract_fusion.3
  724.7 33.9 %all-gather.5.cloned.1.call-done = bf16[2048,1024]{0,1:T(8,128)(2,1)} async-done(((bf16[512,1024]{0,1:T(8,128)(2,1)}), bf16[2048,1024]{0,1:T(8,128)(2,1)}) %all-gather.5.cloned.1.call-update) | async-done | bytes 4194320 | tf_op jit(solution)/shard_map/all_gather | solution.py:39
  758.5 24.2 %convolution_convert_fusion = bf16[1024,4096]{1,0:T(8,128)(2,1)} fusion(bf16[2048,1024]{0,1:T(8,128)(2,1)} %all-gather.5.cloned.1.call-done, bf16[2048,4096]{1,0:T(8,128)(2,1)} %param.4, bf16[2048,4096]{1,0:T(8,128)(2,1)} %param.3), kind=kOutput, calls=%fused_computation.10 | convolution fusion | flops 17217617920 | bytes 46137344 | tf_op jit(solution)/shard_map/dot_general | solution.py:41
  782.7 148.0 %reduce-scatter.5.cloned.1.call-done = bf16[128,4096]{1,0:T(8,128)(2,1)} async-done(((bf16[1024,4096]{1,0:T(8,128)(2,1)}), bf16[128,4096]{1,0:T(8,128)(2,1)}) %reduce-scatter.5.cloned.1.call-update) | async-done | bytes 1048592 | tf_op jit(solution)/shard_map/reduce_scatter | solution.py:40
  932.2 3.2 collective-permute-start.1
  935.5 41.7 %collective-permute-done = bf16[128,4096]{1,0:T(8,128)(2,1)} collective-permute-done((bf16[128,4096]{1,0:T(8,128)(2,1)}, bf16[128,4096]{1,0:T(8,128)(2,1)}, u32[]{:S(2)}, u32[]{:S(2)}) %collective-permute-start) | collective-permute-done | bytes 1048608 | tf_op jit(solution)/shard_map/ppermute | solution.py:59
  983.0 41.0 %collective-permute-done.2 = bf16[128,4096]{1,0:T(8,128)(2,1)S(1)} collective-permute-done((bf16[128,4096]{1,0:T(8,128)(2,1)}, bf16[128,4096]{1,0:T(8,128)(2,1)S(1)}, u32[]{:S(2)}, u32[]{:S(2)}) %collective-permute-start.2) | collective-permute-done | bytes 1048608 | tf_op jit(solution)/shard_map/ppermute | solution.py:59
  1030.3 40.3 %collective-permute-done.4 = bf16[128,4096]{1,0:T(8,128)(2,1)S(1)} collective-permute-done((bf16[128,4096]{1,0:T(8,128)(2,1)S(1)}, bf16[128,4096]{1,0:T(8,128)(2,1)S(1)}, u32[]{:S(2)}, u32[]{:S(2)}) %collective-permute-start.4) | collective-permute-done | bytes 1048608 | tf_op jit(solution)/shard_map/ppermute | solution.py:59
  1073.6 23.3 %collective-permute-done.6 = bf16[128,4096]{1,0:T(8,128)(2,1)S(1)} collective-permute-done((bf16[128,4096]{1,0:T(8,128)(2,1)S(1)}, bf16[128,4096]{1,0:T(8,128)(2,1)S(1)}, u32[]{:S(2)}, u32[]{:S(2)}) %collective-permute-start.6) | collective-permute-done | bytes 1048608 | tf_op jit(solution)/shard_map/ppermute | solution.py:59
  1097.0 3.2 copy-done
  1101.9 5.7 psum.15
  1107.6 25.4 %multiply_convert_fusion = bf16[2048,4096]{1,0:T(8,128)(2,1)} fusion(bf16[2048,1024]{0,1:T(8,128)(2,1)} %all-gather.5.cloned.1.call-done, bf16[1024,4096]{1,0:T(8,128)(2,1)} %copy-done, f32[1024]{0:T(1024)S(1)} %add_rsqrt_fusion), kind=kOutput, calls=%fused_computation.2 | convolution fusion | flops 17209229312 | bytes 29364224 | tf_op jit(solution)/shard_map/dot_general | solution.py:74
  1133.0 31.7 %subtract_convert_fusion = bf16[2048,4096]{1,0:T(8,128)(2,1)} fusion(bf16[2048,1024]{0,1:T(8,128)(2,1)} %all-gather.5.cloned.1.call-done, bf16[1024,4096]{1,0:T(8,128)(2,1)} %copy-done, bf16[2048,4096]{1,0:T(8,128)(2,1)} %param.4, bf16[2048,4096]{1,0:T(8,128)(2,1)} %param.3), kind=kOutput, calls=%fused_computation.3 | convolution fusion | flops 17246978048 | bytes 62914560 | tf_op jit(solution)/shard_map/dot_general | solution.py:73
  (119 shorter events, 88.3 us)
Async XLA Ops:
  7.2 130.2 %all-gather.3.cloned.1.call-start = ((), (), s32[]{:S(2)}) async-start(), calls=%async_computation.2 | async-start | bytes 9437184 | tf_op jit(solution)/shard_map/all_gather | solution.py:30
  7.9 198.2 %reduce-scatter.3.cloned.1.call-start = ((), (), s32[]{:S(2)}) async-start(), calls=%async_computation.3 | async-start | bytes 5242880 | tf_op jit(solution)/shard_map/reduce_scatter | solution.py:34
  163.1 191.5 %all-reduce.3.cloned.1.call-start = ((), (), s32[]{:S(2)}) async-start(), calls=%async_computation.4 | async-start | bytes 8388608 | tf_op jit(solution)/shard_map/psum | solution.py:37
  206.0 5.0 copy-start.1
  211.0 547.5 %all-gather.5.cloned.1.call-start = ((), (), s32[]{:S(2)}) async-start(), calls=%async_computation.5 | async-start | bytes 5242880 | tf_op jit(solution)/shard_map/all_gather | solution.py:39
  364.9 2.0 copy-start.2
  394.9 0.8 copy-start.4
  693.9 7.3 copy-start.5
  724.6 206.1 %reduce-scatter.5.cloned.1.call-start = ((), (), s32[]{:S(2)}) async-start(), calls=%async_computation.6 | async-start | bytes 9437184 | tf_op jit(solution)/shard_map/reduce_scatter | solution.py:40
  930.7 46.4 %collective-permute-start = (bf16[128,4096]{1,0:T(8,128)(2,1)}, bf16[128,4096]{1,0:T(8,128)(2,1)}, u32[]{:S(2)}, u32[]{:S(2)}) collective-permute-start(bf16[128,4096]{1,0:T(8,128)(2,1)} %reduce-scatter.5.cloned.1.call-done), channel_id=1, source_target_pairs={{0,4},{4,8},{8,12},{12,16},{16,20},{20,24},{24,28},{28,0},{1,5},{5... | collective-permute-start | bytes 3145736 | tf_op jit(solution)/shard_map/ppermute | solution.py:59
  932.2 47.4 %collective-permute-start.1 = (bf16[128,4096]{1,0:T(8,128)(2,1)}, bf16[128,4096]{1,0:T(8,128)(2,1)S(1)}, u32[]{:S(2)}, u32[]{:S(2)}) collective-permute-start(bf16[128,4096]{1,0:T(8,128)(2,1)} %reduce-scatter.5.cloned.1.call-done), channel_id=1, source_target_pairs={{0,28},{4,0},{8,4},{12,8},{16,12},{20,16},{24,20},{28,24},{1,29},{... | collective-permute-start | bytes 3145736 | tf_op jit(solution)/shard_map/ppermute | solution.py:64
  977.1 46.9 %collective-permute-start.2 = (bf16[128,4096]{1,0:T(8,128)(2,1)}, bf16[128,4096]{1,0:T(8,128)(2,1)S(1)}, u32[]{:S(2)}, u32[]{:S(2)}) collective-permute-start(bf16[128,4096]{1,0:T(8,128)(2,1)} %collective-permute-done), channel_id=1, source_target_pairs={{0,4},{4,8},{8,12},{12,16},{16,20},{20,24},{24,28},{28,0},{1,5},{5... | collective-permute-start | bytes 3145736 | tf_op jit(solution)/shard_map/ppermute | solution.py:59
  979.6 3.3 copy-start.3
  979.6 48.2 %collective-permute-start.3 = (bf16[128,4096]{1,0:T(8,128)(2,1)S(1)}, bf16[128,4096]{1,0:T(8,128)(2,1)S(1)}, u32[]{:S(2)}, u32[]{:S(2)}) collective-permute-start(bf16[128,4096]{1,0:T(8,128)(2,1)S(1)} %collective-permute-done.1), channel_id=1, source_target_pairs={{0,28},{4,0},{8,4},{12,8},{16,12},{20,16},{24,20},{28,24},{1,29},{... | collective-permute-start | bytes 3145736 | tf_op jit(solution)/shard_map/ppermute | solution.py:64
  1024.0 46.7 %collective-permute-start.4 = (bf16[128,4096]{1,0:T(8,128)(2,1)S(1)}, bf16[128,4096]{1,0:T(8,128)(2,1)S(1)}, u32[]{:S(2)}, u32[]{:S(2)}) collective-permute-start(bf16[128,4096]{1,0:T(8,128)(2,1)S(1)} %collective-permute-done.2), channel_id=1, source_target_pairs={{0,4},{4,8},{8,12},{12,16},{16,20},{20,24},{24,28},{28,0},{1,5},{5... | collective-permute-start | bytes 3145736 | tf_op jit(solution)/shard_map/ppermute | solution.py:59
  1027.8 45.6 %collective-permute-start.5 = (bf16[128,4096]{1,0:T(8,128)(2,1)S(1)}, bf16[128,4096]{1,0:T(8,128)(2,1)S(1)}, u32[]{:S(2)}, u32[]{:S(2)}) collective-permute-start(bf16[128,4096]{1,0:T(8,128)(2,1)S(1)} %collective-permute-done.3), channel_id=1, source_target_pairs={{0,28},{4,0},{8,4},{12,8},{16,12},{20,16},{24,20},{28,24},{1,29},{... | collective-permute-start | bytes 3145736 | tf_op jit(solution)/shard_map/ppermute | solution.py:64
  1070.7 26.2 %collective-permute-start.6 = (bf16[128,4096]{1,0:T(8,128)(2,1)S(1)}, bf16[128,4096]{1,0:T(8,128)(2,1)S(1)}, u32[]{:S(2)}, u32[]{:S(2)}) collective-permute-start(bf16[128,4096]{1,0:T(8,128)(2,1)S(1)} %collective-permute-done.4), channel_id=1, source_target_pairs={{0,4},{4,8},{8,12},{12,16},{16,20},{20,24},{24,28},{28,0},{1,5},{5... | collective-permute-start | bytes 3145736 | tf_op jit(solution)/shard_map/ppermute | solution.py:59
  1097.0 3.2 copy-start
Sparse Core Ops, SparseCore 0:
  10.1 127.1 all-gather.2
  163.3 42.7 reduce-scatter.2
  212.2 142.4 all-reduce.2
  724.7 33.7 all-gather.4
  782.8 147.8 reduce-scatter.4
